TPU v7x, 256 devices: a whole 4x4x8 slice. The times are simulated.
256 devices in a mesh: dom: 64 (over x, z, y_hi), head: 4 (over y_lo, core).
Axes of the slice: x: 4, y: 4 (y_hi: 2, y_lo: 2; y = y_hi * 2 + y_lo), z: 8, core: 2. Of those that a mesh axis runs over, the one named last changes fastest.
Arguments:
- vertex_embeddings: bfloat16 [32768, 512], P(('dom', 'head')), may hold values from -6 to 6
- adjacent_group_bank_ids: int32 [64, 4, 12], P('dom', 'head'), may hold values from -1 to 15, as said below
- coupling_strength_panels: bfloat16 [16, 128, 128], replicated, may hold values from -0.3125 to 0.3125
- asking_projector: bfloat16 [512, 512], replicated, may hold values from -0.25 to 0.25
- lookup_projector: bfloat16 [512, 512], replicated, may hold values from -0.25 to 0.25
- content_projector: bfloat16 [512, 512], replicated, may hold values from -0.25 to 0.25
- final_projector: bfloat16 [512, 512], replicated, may hold values from -0.25 to 0.25
- passing_inner_coefficients: bfloat16 [512, 1024], replicated, may hold values from -0.25 to 0.25
- passing_outer_coefficients: bfloat16 [1024, 512], replicated, may hold values from -0.1875 to 0.1875
- softness_per_subspace: float32 [8], replicated, may hold values from 0.5 to 2
- mixing_layer_gain: float32 [512], replicated, may hold values from 0.5 to 1.5
Outputs:
- result: bfloat16 [32768, 512], P(('dom', 'head'))
Inputs may be any that keep to these rules, and one draw needn't show every extreme that they name: `adjacent_group_bank_ids`: -1 marks a block without edges. The entry of a block for itself is never -1, nor is at least one entry for each neighbouring partition.
All inputs are finite; a program needn't handle non-finite values.
Results may differ from a plain program's by a relative error of at most 0.0054.
Values may be sent and summed in bfloat16 or wider, within the bound.
A program may use at most 64 MiB of HBM per device.

v0:
```python
import math
import jax
import jax.numpy as jnp
from jax import lax
from jax.sharding import PartitionSpec as P

NUM_SUBSPACES = 8
SUBSPACE_WIDTH = 64
norm_eps = 1e-06


def extended(shard, sides, width):
    for axis, dim in sides:
        devices, length = (lax.axis_size(axis), shard.shape[dim])
        up = [(i, (i + 1) % devices) for i in range(devices - 1)]
        down = [(j, i) for i, j in up]
        last = lax.slice_in_dim(shard, length - width, length, axis=dim)
        first = lax.slice_in_dim(shard, 0, width, axis=dim)
        before = lax.ppermute(last, axis, up)
        after = lax.ppermute(first, axis, down)
        shard = jnp.concatenate([before, shard, after], axis=dim)
    return shard


def head_norm(projected, scales):
    rows = projected.shape[0]
    grouped = projected.reshape(rows, -1, SUBSPACE_WIDTH)
    mean_square = jnp.mean(grouped * grouped, axis=-1, keepdims=True)
    scaled = grouped * lax.rsqrt(mean_square + norm_eps)
    if scales is not None:
        scaled = scaled * scales[None, :, None]
    return scaled.reshape(rows, -1).astype(jnp.bfloat16)


def shards(
    vertex_embeddings,
    adjacent_group_bank_ids,
    coupling_strength_panels,
    asking_projector,
    lookup_projector,
    content_projector,
    final_projector,
    passing_inner_coefficients,
    passing_outer_coefficients,
    softness_per_subspace,
    mixing_layer_gain,
):
    block_len = vertex_embeddings.shape[0]
    group_size = lax.axis_size("head")
    heads_here = NUM_SUBSPACES // group_size
    head_cols = heads_here * SUBSPACE_WIDTH
    slot_ids = adjacent_group_bank_ids.reshape(-1)
    halo_rows = extended(vertex_embeddings, (("dom", 0),), block_len)
    nearby = lax.all_gather(halo_rows, "head", axis=0, tiled=True)
    slot_order = slot_ids.reshape(3, group_size).T.reshape(-1)
    asking_vector_multiplier = softness_per_subspace / math.sqrt(SUBSPACE_WIDTH)
    queries = head_norm(
        jnp.dot(vertex_embeddings, asking_projector, preferred_element_type=jnp.float32),
        asking_vector_multiplier,
    )
    keys_all = head_norm(
        jnp.dot(vertex_embeddings, lookup_projector, preferred_element_type=jnp.float32), None
    )
    values_all = jnp.dot(
        vertex_embeddings, content_projector, preferred_element_type=jnp.float32
    ).astype(jnp.bfloat16)
    queries, keys_all, values_all = (
        lax.all_to_all(queries, "head", split_axis=1, concat_axis=0, tiled=True),
        lax.all_to_all(keys_all, "head", split_axis=1, concat_axis=0, tiled=True),
        lax.all_to_all(values_all, "head", split_axis=1, concat_axis=0, tiled=True),
    )
    selected = jnp.take(coupling_strength_panels, jnp.maximum(slot_order, 0), axis=0)
    selected = jnp.where((slot_order >= 0)[:, None, None], selected, jnp.zeros_like(selected))
    wide_tiles = jnp.transpose(selected, (1, 0, 2)).reshape(block_len, -1)
    aggregate = jnp.dot(wide_tiles, nearby, preferred_element_type=jnp.float32).astype(jnp.bfloat16)
    hidden = jax.nn.gelu(
        jnp.dot(aggregate, passing_inner_coefficients, preferred_element_type=jnp.float32)
    ).astype(jnp.bfloat16)
    local_term = jnp.dot(hidden, passing_outer_coefficients, preferred_element_type=jnp.float32)
    query_rows = queries.shape[0]
    start_totals = (
        jnp.zeros((query_rows, head_cols), jnp.float32),
        jnp.zeros((query_rows, heads_here), jnp.float32),
    )
    keys_in = lax.all_gather(keys_all, "dom", axis=0, tiled=True)
    values_in = lax.all_gather(values_all, "dom", axis=0, tiled=True)
    key_count = keys_in.shape[0]
    block_step = key_count
    while block_step > 2048 and block_step % 2 == 0:
        block_step = block_step // 2

    def accumulate(turn_index, totals):
        numerator, denominator = totals
        key_block = lax.dynamic_slice_in_dim(keys_in, turn_index * block_step, block_step, 0)
        value_block = lax.dynamic_slice_in_dim(values_in, turn_index * block_step, block_step, 0)
        new_numer = []
        new_denom = []
        for head_id in range(heads_here):
            cols = slice(head_id * SUBSPACE_WIDTH, (head_id + 1) * SUBSPACE_WIDTH)
            scores = jnp.einsum(
                "qd,kd->qk",
                queries[:, cols],
                key_block[:, cols],
                preferred_element_type=jnp.float32,
            )
            weights = jnp.exp(scores).astype(jnp.bfloat16)
            new_denom.append(jnp.sum(weights, axis=1, dtype=jnp.float32))
            new_numer.append(
                jnp.dot(weights, value_block[:, cols], preferred_element_type=jnp.float32)
            )
        return (
            numerator + jnp.concatenate(new_numer, axis=1),
            denominator + jnp.stack(new_denom, axis=1),
        )

    numerator, denominator = lax.fori_loop(0, key_count // block_step, accumulate, start_totals)
    merged = (
        (numerator.reshape(query_rows, heads_here, SUBSPACE_WIDTH) / denominator[:, :, None])
        .reshape(query_rows, head_cols)
        .astype(jnp.bfloat16)
    )
    node_heads = lax.all_to_all(merged, "head", split_axis=0, concat_axis=1, tiled=True)
    attended = jnp.dot(node_heads, final_projector, preferred_element_type=jnp.float32)
    normed = (
        attended
        * lax.rsqrt(jnp.mean(attended * attended, axis=-1, keepdims=True) + norm_eps)
        * mixing_layer_gain
    )
    return (vertex_embeddings.astype(jnp.float32) + local_term + normed).astype(jnp.bfloat16)


def solution(mesh):
    in_specs = (
        P(("dom", "head"), None),
        P("dom", "head", None),
        P(),
        P(),
        P(),
        P(),
        P(),
        P(),
        P(),
        P(),
        P(),
    )
    out_specs = P(("dom", "head"), None)
    return jax.shard_map(shards, mesh=mesh, in_specs=in_specs, out_specs=out_specs, check_vma=False)
```

profile of v0, /device:TPU:1, one launch (start us, length us, event | category | flops | bytes accessed | tf_op | source)
XLA Modules:
  0.0 446.1 jit_solution(16894264735324568818)
XLA Ops:
  8.4 9.9 %all_to_all.76 = bf16[128,4,128]{2,0,1:T(8,128)(2,1)} all-to-all(bf16[128,4,128]{2,0,1:T(8,128)(2,1)S(1)} %copy_bitcast_fusion.2), channel_id=1, replica_groups=mesh['dom'=64,'head'=4] {'head'}, dimensions={1} | all-to-all | bytes 262144 | tf_op jit(solution)/shard_map/all_to_all | solution.py:69
  19.8 7.7 %all_to_all.77 = bf16[128,4,128]{2,0,1:T(8,128)(2,1)} all-to-all(bf16[128,4,128]{2,0,1:T(8,128)(2,1)S(1)} %bitcast.74), channel_id=1, replica_groups=mesh['dom'=64,'head'=4] {'head'}, dimensions={1} | all-to-all | bytes 262144 | tf_op jit(solution)/shard_map/all_to_all | solution.py:70
  27.5 3.1 collective-permute-start
  33.3 4.6 %all-to-all-start.1 = ((bf16[128,4,128]{2,0,1:T(8,128)(2,1)}), bf16[128,4,128]{2,0,1:T(8,128)(2,1)S(1)}, u32[]{:S(2)}, u32[]{:S(2)}) async-start(bf16[128,4,128]{2,0,1:T(8,128)(2,1)} %copy_bitcast_fusion.1), calls=%async_computation.1 | async-start | bytes 262144 | tf_op jit(solution)/shard_map/all_to_all | solution.py:68
  42.0 122.8 %all-gather.6.cloned.1.call-done = bf16[32768,128]{1,0:T(8,128)(2,1)} async-done(((bf16[512,128]{1,0:T(8,128)(2,1)}), bf16[32768,128]{1,0:T(8,128)(2,1)}) %all-gather.6.cloned.1.call-update) | async-done | bytes 8388624 | tf_op jit(solution)/shard_map/all_gather | solution.py:85
  164.7 147.5 %all-gather.8.cloned.1.call-done = bf16[32768,128]{1,0:T(8,128)(2,1)} async-done(((bf16[512,128]{1,0:T(8,128)(2,1)}), bf16[32768,128]{1,0:T(8,128)(2,1)}) %all-gather.8.cloned.1.call-update) | async-done | bytes 8388624 | tf_op jit(solution)/shard_map/all_gather | solution.py:86
  312.2 114.2 %while.16 = (s32[]{:T(128)}, f32[512,128]{0,1:T(8,128)S(1)}, f32[512,2]{0,1:T(2,128)S(1)}, bf16[32768,128]{1,0:T(8,128)(2,1)}, bf16[512,128]{1,0:T(8,128)(2,1)S(...) while((s32[]{:T(128)}, f32[512,128]{0,1:T(8,128)S(1)}, ...), condition=%wide.region_5.6_spmd.clone, body=%wide.region_2.5_spmd.clone.sunk | while | flops 543361024 | bytes 11813066 | solution.py:116
  312.2 1.9 convert_reduce_fusion.4
  315.9 1.8 convert_reduce_fusion.5
  319.3 1.9 convert_reduce_fusion.4
  323.0 1.8 convert_reduce_fusion.5
  326.5 1.9 convert_reduce_fusion.4
  328.4 1.7 fusion.54
  330.2 1.8 convert_reduce_fusion.5
  333.7 1.9 convert_reduce_fusion.4
  335.6 1.7 fusion.54
  337.3 1.8 convert_reduce_fusion.5
  340.8 1.9 convert_reduce_fusion.4
  342.7 1.7 fusion.54
  344.5 1.8 convert_reduce_fusion.5
  347.9 1.9 convert_reduce_fusion.4
  349.9 1.7 fusion.54
  351.6 1.8 convert_reduce_fusion.5
  355.1 1.9 convert_reduce_fusion.4
  357.0 1.7 fusion.54
  358.7 1.8 convert_reduce_fusion.5
  362.2 1.9 convert_reduce_fusion.4
  364.1 1.7 fusion.54
  365.9 1.8 convert_reduce_fusion.5
  369.3 1.9 convert_reduce_fusion.4
  373.0 1.8 convert_reduce_fusion.5
  376.5 1.9 convert_reduce_fusion.4
  380.1 1.8 convert_reduce_fusion.5
  383.6 1.9 convert_reduce_fusion.4
  387.2 1.8 convert_reduce_fusion.5
  390.7 1.9 convert_reduce_fusion.4
  394.4 1.8 convert_reduce_fusion.5
  397.9 1.9 convert_reduce_fusion.4
  401.5 1.8 convert_reduce_fusion.5
  405.0 1.9 convert_reduce_fusion.4
  408.6 1.8 convert_reduce_fusion.5
  412.1 1.9 convert_reduce_fusion.4
  415.8 1.8 convert_reduce_fusion.5
  419.3 1.9 convert_reduce_fusion.4
  422.9 1.8 convert_reduce_fusion.5
  427.2 6.4 %all-to-all-start.3 = ((bf16[4,128,128]{2,1,0:T(8,128)(2,1)}), bf16[4,128,128]{2,1,0:T(8,128)(2,1)S(1)}, u32[]{:S(2)}, u32[]{:S(2)}) async-start(bf16[4,128,128]{2,1,0:T(8,128)(2,1)} %bitcast.16), calls=%async_computation.3 | async-start | bytes 262144 | tf_op jit(solution)/shard_map/all_to_all | solution.py:122
  433.6 2.8 fusion.21
  437.7 1.9 fusion.11
  (130 shorter events, 55.8 us)
Async XLA Ops:
  6.5 427.0 %copy-start = (bf16[512,1024]{1,0:T(8,128)(2,1)S(1)}, bf16[512,1024]{1,0:T(8,128)(2,1)}, u32[]{:S(2)}) copy-start(bf16[512,1024]{1,0:T(8,128)(2,1)} %param.20) | copy-start | bytes 3145732
  6.5 20.9 %copy-start.1 = (bf16[128,512]{1,0:T(8,128)(2,1)S(1)}, bf16[128,512]{1,0:T(8,128)(2,1)}, u32[]{:S(2)}) copy-start(bf16[128,512]{1,0:T(8,128)(2,1)} %param.13) | copy-start | bytes 393220
  6.5 25.4 %copy-start.3 = (bf16[512,512]{1,0:T(8,128)(2,1)S(1)}, bf16[512,512]{1,0:T(8,128)(2,1)}, u32[]{:S(2)}) copy-start(bf16[512,512]{1,0:T(8,128)(2,1)} %param.16) | copy-start | bytes 1572868
  6.5 25.9 %copy-start.7 = (f32[8]{0:T(128)S(1)}, f32[8]{0:T(128)}, u32[]{:S(2)}) copy-start(f32[8]{0:T(128)} %param.22) | copy-start | bytes 100
  6.5 158.2 %all-gather.6.cloned.1.call-start = ((), (), s32[]{:S(2)}) async-start(), calls=%async_computation.5 | async-start | bytes 8519680 | tf_op jit(solution)/shard_map/all_gather | solution.py:85
  8.0 29.9 %copy-start.8 = (s32[1,1,12]{2,1,0:T(1,128)S(1)}, s32[1,1,12]{2,1,0:T(1,128)}, u32[]{:S(2)}) copy-start(s32[1,1,12]{2,1,0:T(1,128)} %param.14) | copy-start | bytes 148
  8.1 30.8 %copy-start.5 = (bf16[16,128,128]{2,1,0:T(8,128)(2,1)S(1)}, bf16[16,128,128]{2,1,0:T(8,128)(2,1)}, u32[]{:S(2)}) copy-start(bf16[16,128,128]{2,1,0:T(8,128)(2,1)} %param.15) | copy-start | bytes 1572868
  18.3 293.9 %all-gather.8.cloned.1.call-start = ((), (), s32[]{:S(2)}) async-start(), calls=%async_computation.6 | async-start | bytes 8519680 | tf_op jit(solution)/shard_map/all_gather | solution.py:86
  27.5 12.4 %collective-permute-start = (bf16[128,512]{1,0:T(8,128)(2,1)S(1)}, bf16[128,512]{1,0:T(8,128)(2,1)S(1)}, u32[]{:S(2)}, u32[]{:S(2)}) collective-permute-start(bf16[128,512]{1,0:T(8,128)(2,1)S(1)} %copy-done.1), channel_id=1, source_target_pairs={{0,4},{4,8},{8,12},{12,16},{16,20},{20,24},{24,28},{28,32},{32,36}... | collective-permute-start | bytes 393224 | tf_op jit(solution)/shard_map/ppermute | solution.py:19
  30.6 9.3 %collective-permute-start.1 = (bf16[128,512]{1,0:T(8,128)(2,1)S(1)}, bf16[128,512]{1,0:T(8,128)(2,1)S(1)}, u32[]{:S(2)}, u32[]{:S(2)}) collective-permute-start(bf16[128,512]{1,0:T(8,128)(2,1)S(1)} %copy-done.1), channel_id=1, source_target_pairs={{4,0},{8,4},{12,8},{16,12},{20,16},{24,20},{28,24},{32,28},{36,32}... | collective-permute-start | bytes 393224 | tf_op jit(solution)/shard_map/ppermute | solution.py:20
  33.3 8.6 %all-to-all-start.1 = ((bf16[128,4,128]{2,0,1:T(8,128)(2,1)}), bf16[128,4,128]{2,0,1:T(8,128)(2,1)S(1)}, u32[]{:S(2)}, u32[]{:S(2)}) async-start(bf16[128,4,128]{2,0,1:T(8,128)(2,1)} %copy_bitcast_fusion.1), calls=%async_computation.1 | async-start | bytes 262144 | tf_op jit(solution)/shard_map/all_to_all | solution.py:68
  38.0 395.6 %all-gather.4.cloned.1.call-start = ((), (), s32[]{:S(2)}) async-start(), calls=%async_computation.4 | async-start | bytes 1966080 | tf_op jit(solution)/shard_map/all_gather | solution.py:54
  426.4 10.9 %copy-start.4 = (bf16[512,512]{1,0:T(8,128)(2,1)S(1)}, bf16[512,512]{1,0:T(8,128)(2,1)}, u32[]{:S(2)}) copy-start(bf16[512,512]{1,0:T(8,128)(2,1)} %param.19) | copy-start | bytes 1572868
  426.4 11.3 %copy-start.2 = (bf16[1024,512]{1,0:T(8,128)(2,1)S(1)}, bf16[1024,512]{1,0:T(8,128)(2,1)}, u32[]{:S(2)}) copy-start(bf16[1024,512]{1,0:T(8,128)(2,1)} %param.21) | copy-start | bytes 3145732
  426.4 11.3 %copy-start.6 = (f32[512]{0:T(512)S(1)}, f32[512]{0:T(512)}, u32[]{:S(2)}) copy-start(f32[512]{0:T(512)} %param.23) | copy-start | bytes 6148
  427.2 10.0 %all-to-all-start.3 = ((bf16[4,128,128]{2,1,0:T(8,128)(2,1)}), bf16[4,128,128]{2,1,0:T(8,128)(2,1)S(1)}, u32[]{:S(2)}, u32[]{:S(2)}) async-start(bf16[4,128,128]{2,1,0:T(8,128)(2,1)} %bitcast.16), calls=%async_computation.3 | async-start | bytes 262144 | tf_op jit(solution)/shard_map/all_to_all | solution.py:122
Sparse Core Ops, SparseCore 0:
  18.5 146.2 all-gather.5
  168.3 143.8 all-gather.7
  314.0 26.9 all-gather.3
where the time goes:
time: 450 us; the launch traced here: 446 us
  waiting for transfers between devices  272 us (60%)
  matrix products  120 us (27%)
  blocking collectives  17.5 us (4%)
  starting transfers between devices  15.4 us (3%)
  between operations  13.4 us (3%)
    all_gather x1, waiting for transfers between devices, shards(): values_in = lax.all_gather(values_all, 'dom', axis=0, tiled=True)  147 us
    all_gather x1, waiting for transfers between devices, shards(): keys_in = lax.all_gather(keys_all, 'dom', axis=0, tiled=True)  123 us
    dot_general x32, matrix products, accumulate(): jnp.einsum('qd,kd->qk', queries[:, cols], key_block[:, cols], preferred_e...  59.1 us
    dot_general x32, matrix products, accumulate(): jnp.dot(weights, value_block[:, cols], preferred_element_type=jnp.float32)  52.5 us
    all_to_all x1, blocking collectives, shards(): lax.all_to_all(keys_all, 'head', split_axis=1, concat_axis=0, tiled=True)  9.87 us
  transfers between devices with their start and end apart: 7, of which 4 were waited for; matrix products, arithmetic and copies ran while one was open for 27% of the time, Pallas kernels for 0%

commit v1 on v0

--- a/solution.py
+++ b/solution.py
@@ -83,7 +83,9 @@
         jnp.zeros((query_rows, heads_here), jnp.float32),
     )
     keys_in = lax.all_gather(keys_all, "dom", axis=0, tiled=True)
-    values_in = lax.all_gather(values_all, "dom", axis=0, tiled=True)
+    values_in = jnp.concatenate(
+        lax.all_to_all(jnp.stack([values_all] * lax.axis_size("dom")), "dom", 0, 0), axis=0
+    )
     key_count = keys_in.shape[0]
     block_step = key_count
     while block_step > 2048 and block_step % 2 == 0:

time: 450 us -> 412 us (0.916)
  waiting for transfers between devices: 272 us -> 221 us
  starting transfers between devices: 15.4 us -> 38 us
  blocking collectives: 17.5 us -> 0 us
  local copies, waits for them, and re-layouts: 3.34 us -> 9.24 us
    all_gather x1 -> x0, waiting for transfers between devices: 147 us -> none  [shards(): values_in = lax.all_gather(values_all, 'dom', axis=0, tiled=True)]
    all_gather x1, waiting for transfers between devices: 123 us -> 195 us  [shards(): keys_in = lax.all_gather(keys_all, 'dom', axis=0, tiled=True)]
    all_to_all x0 -> x3, starting transfers between devices: none -> 21.6 us  [the longest x1 12.9 us: shards(): lax.all_to_all(jnp.stack([values_all] * lax.axis_size('dom')), 'dom', 0, 0)]
    all_to_all x2 -> x0, blocking collectives: 17.5 us -> none  [the longest x1 9.87 us: shards(): lax.all_to_all(keys_all, 'head', split_axis=1, concat_axis=0, tiled=True)]
    ppermute x1, waiting for transfers between devices: 0.01 us -> 11.8 us  [extended(): before = lax.ppermute(last, axis, up)]
    ppermute x1, waiting for transfers between devices: 0.01 us -> 5.55 us  [extended(): after = lax.ppermute(first, axis, down)]
    all_to_all x0 -> x3, waiting for transfers between devices: none -> 5.55 us  [the longest x1 2.88 us: shards(): lax.all_to_all(values_all, 'head', split_axis=1, concat_axis=0, tiled=True)]
    another operation x0 -> x1, local copies, waits for them, and re-layouts: none -> 5.24 us  [shards(): jnp.stack([values_all] * lax.axis_size('dom'))]
  transfers between devices with their start and end apart: 7 -> 9, of which waited for: 4 -> 7; matrix products, arithmetic and copies ran while one was open for 27% -> 31% of each run, Pallas kernels for 0% -> 0%
where the time goes in v1:
time: 412 us; the launch traced here: 407 us
  waiting for transfers between devices  221 us (54%)
  matrix products  120 us (29%)
  starting transfers between devices  38 us (9%)
  between operations  13.7 us (3%)
  local copies, waits for them, and re-layouts  9.24 us (2%)
  other arithmetic  4.78 us (1%)
    all_gather x1, waiting for transfers between devices, shards(): keys_in = lax.all_gather(keys_all, 'dom', axis=0, tiled=True)  195 us
    dot_general x32, matrix products, accumulate(): jnp.einsum('qd,kd->qk', queries[:, cols], key_block[:, cols], preferred_e...  59 us
    dot_general x32, matrix products, accumulate(): jnp.dot(weights, value_block[:, cols], preferred_element_type=jnp.float32)  52.6 us
    all_to_all x1, starting transfers between devices, shards(): lax.all_to_all(jnp.stack([values_all] * lax.axis_size('dom')), 'dom', 0, 0)  12.9 us
    ppermute x1, waiting for transfers between devices, extended(): before = lax.ppermute(last, axis, up)  11.8 us
  transfers between devices with their start and end apart: 9, of which 7 were waited for; matrix products, arithmetic and copies ran while one was open for 31% of the time, Pallas kernels for 0%

profile of v1, /device:TPU:1, one launch (start us, length us, event | category | flops | bytes accessed | tf_op | source)
XLA Modules:
  0.0 407.0 jit_solution(6640386290506742570)
XLA Ops:
  9.8 6.5 %all-to-all-start.1 = ((bf16[128,4,128]{2,0,1:T(8,128)(2,1)}), bf16[128,4,128]{2,0,1:T(8,128)(2,1)S(1)}, u32[]{:S(2)}, u32[]{:S(2)}) async-start(bf16[128,4,128]{2,0,1:T(8,128)(2,1)} %copy_bitcast_fusion.1), calls=%async_computation.1 | async-start | bytes 262144 | tf_op jit(solution)/shard_map/all_to_all | solution.py:68
  20.0 4.3 %all-to-all-start = ((bf16[128,4,128]{2,0,1:T(8,128)(2,1)}), bf16[128,4,128]{2,0,1:T(8,128)(2,1)S(1)}, u32[]{:S(2)}, u32[]{:S(2)}) async-start(bf16[128,4,128]{2,0,1:T(8,128)(2,1)} %copy_bitcast_fusion.2), calls=%async_computation | async-start | bytes 262144 | tf_op jit(solution)/shard_map/all_to_all | solution.py:69
  25.2 2.7 all-to-all-done
  27.9 4.3 %all-to-all-start.2 = ((bf16[128,4,128]{2,0,1:T(8,128)(2,1)}), bf16[128,4,128]{2,0,1:T(8,128)(2,1)S(1)}, u32[]{:S(2)}, u32[]{:S(2)}) async-start(bf16[128,4,128]{2,0,1:T(8,128)(2,1)} %bitcast.60), calls=%async_computation.2 | async-start | bytes 262144 | tf_op jit(solution)/shard_map/all_to_all | solution.py:70
  33.0 2.9 all-to-all-done.2
  35.8 5.2 %stack.23 = bf16[64,512,128]{2,1,0:T(8,128)(2,1)} broadcast(bf16[512,128]{1,0:T(8,128)(2,1)S(1)} %bitcast.71), dimensions={1,2} | broadcast | bytes 8519680 | tf_op jit(solution)/shard_map/stack | solution.py:87
  41.1 12.9 %all-to-all-start.3 = ((bf16[64,512,128]{2,1,0:T(8,128)(2,1)}), bf16[64,512,128]{2,1,0:T(8,128)(2,1)}, u32[]{:S(2)}, u32[]{:S(2)}) async-start(bf16[64,512,128]{2,1,0:T(8,128)(2,1)} %stack.23), calls=%async_computation.3 | async-start | bytes 16777216 | tf_op jit(solution)/shard_map/all_to_all | solution.py:87
  54.1 4.4 %collective-permute-start = (bf16[128,512]{1,0:T(8,128)(2,1)S(1)}, bf16[128,512]{1,0:T(8,128)(2,1)S(1)}, u32[]{:S(2)}, u32[]{:S(2)}) collective-permute-start(bf16[128,512]{1,0:T(8,128)(2,1)S(1)} %copy-done.1), channel_id=1, source_target_pairs={{0,4},{4,8},{8,12},{12,16},{16,20},{20,24},{24,28},{28,32},{32,36}... | collective-permute-start | bytes 393224 | tf_op jit(solution)/shard_map/ppermute | solution.py:19
  61.7 11.8 %collective-permute-done = bf16[128,512]{1,0:T(8,128)(2,1)S(1)} collective-permute-done((bf16[128,512]{1,0:T(8,128)(2,1)S(1)}, bf16[128,512]{1,0:T(8,128)(2,1)S(1)}, u32[]{:S(2)}, u32[]{:S(2)}) %collective-permute-start) | collective-permute-done | bytes 131104 | tf_op jit(solution)/shard_map/ppermute | solution.py:19
  73.5 5.6 %collective-permute-done.1 = bf16[128,512]{1,0:T(8,128)(2,1)S(1)} collective-permute-done((bf16[128,512]{1,0:T(8,128)(2,1)S(1)}, bf16[128,512]{1,0:T(8,128)(2,1)S(1)}, u32[]{:S(2)}, u32[]{:S(2)}) %collective-permute-start.1) | collective-permute-done | bytes 131104 | tf_op jit(solution)/shard_map/ppermute | solution.py:20
  79.8 195.2 %all-gather.5.cloned.1.call-done = bf16[32768,128]{1,0:T(8,128)(2,1)} async-done(((bf16[512,128]{1,0:T(8,128)(2,1)}), bf16[32768,128]{1,0:T(8,128)(2,1)}) %all-gather.5.cloned.1.call-update) | async-done | bytes 8388624 | tf_op jit(solution)/shard_map/all_gather | solution.py:85
  275.0 114.0 %while.16 = (s32[]{:T(128)}, f32[512,128]{0,1:T(8,128)S(1)}, f32[512,2]{0,1:T(2,128)S(1)}, bf16[32768,128]{1,0:T(8,128)(2,1)}, bf16[512,128]{1,0:T(8,128)(2,1)S(...) while((s32[]{:T(128)}, f32[512,128]{0,1:T(8,128)S(1)}, ...), condition=%wide.region_5.6_spmd.clone, body=%wide.region_2.5_spmd.clone.sunk | while | flops 543361024 | bytes 11813066 | solution.py:118
  275.0 1.9 convert_reduce_fusion.4
  278.6 1.8 convert_reduce_fusion.5
  282.1 1.9 convert_reduce_fusion.4
  285.7 1.8 convert_reduce_fusion.5
  289.2 1.9 convert_reduce_fusion.4
  292.9 1.8 convert_reduce_fusion.5
  296.4 1.9 convert_reduce_fusion.4
  298.3 1.7 fusion.54
  300.1 1.8 convert_reduce_fusion.5
  303.5 1.9 convert_reduce_fusion.4
  307.2 1.8 convert_reduce_fusion.5
  310.7 1.9 convert_reduce_fusion.4
  314.3 1.8 convert_reduce_fusion.5
  317.8 1.9 convert_reduce_fusion.4
  321.4 1.8 convert_reduce_fusion.5
  324.9 1.9 convert_reduce_fusion.4
  328.6 1.8 convert_reduce_fusion.5
  332.0 1.9 convert_reduce_fusion.4
  335.7 1.8 convert_reduce_fusion.5
  339.2 1.9 convert_reduce_fusion.4
  342.8 1.8 convert_reduce_fusion.5
  346.3 1.9 convert_reduce_fusion.4
  349.9 1.8 convert_reduce_fusion.5
  353.4 1.9 convert_reduce_fusion.4
  357.1 1.8 convert_reduce_fusion.5
  360.5 1.9 convert_reduce_fusion.4
  364.2 1.8 convert_reduce_fusion.5
  367.7 1.9 convert_reduce_fusion.4
  371.3 1.8 convert_reduce_fusion.5
  374.8 1.9 convert_reduce_fusion.4
  378.4 1.8 convert_reduce_fusion.5
  381.9 1.9 convert_reduce_fusion.4
  385.6 1.8 convert_reduce_fusion.5
  389.8 4.2 %all-to-all-start.4 = ((bf16[4,128,128]{2,1,0:T(8,128)(2,1)}), bf16[4,128,128]{2,1,0:T(8,128)(2,1)S(1)}, u32[]{:S(2)}, u32[]{:S(2)}) async-start(bf16[4,128,128]{2,1,0:T(8,128)(2,1)} %bitcast.17), calls=%async_computation.4 | async-start | bytes 262144 | tf_op jit(solution)/shard_map/all_to_all | solution.py:124
  394.1 2.8 fusion.21
  398.2 1.9 fusion.11
  (132 shorter events, 67.1 us)
Async XLA Ops:
  6.5 387.5 %copy-start = (bf16[512,1024]{1,0:T(8,128)(2,1)S(1)}, bf16[512,1024]{1,0:T(8,128)(2,1)}, u32[]{:S(2)}) copy-start(bf16[512,1024]{1,0:T(8,128)(2,1)} %param.20) | copy-start | bytes 3145732
  6.5 17.8 %copy-start.1 = (bf16[128,512]{1,0:T(8,128)(2,1)S(1)}, bf16[128,512]{1,0:T(8,128)(2,1)}, u32[]{:S(2)}) copy-start(bf16[128,512]{1,0:T(8,128)(2,1)} %param.13) | copy-start | bytes 393220
  6.5 17.8 %copy-start.3 = (bf16[512,512]{1,0:T(8,128)(2,1)S(1)}, bf16[512,512]{1,0:T(8,128)(2,1)}, u32[]{:S(2)}) copy-start(bf16[512,512]{1,0:T(8,128)(2,1)} %param.18) | copy-start | bytes 1572868
  9.8 10.1 %all-to-all-start.1 = ((bf16[128,4,128]{2,0,1:T(8,128)(2,1)}), bf16[128,4,128]{2,0,1:T(8,128)(2,1)S(1)}, u32[]{:S(2)}, u32[]{:S(2)}) async-start(bf16[128,4,128]{2,0,1:T(8,128)(2,1)} %copy_bitcast_fusion.1), calls=%async_computation.1 | async-start | bytes 262144 | tf_op jit(solution)/shard_map/all_to_all | solution.py:68
  20.0 7.9 %all-to-all-start = ((bf16[128,4,128]{2,0,1:T(8,128)(2,1)}), bf16[128,4,128]{2,0,1:T(8,128)(2,1)S(1)}, u32[]{:S(2)}, u32[]{:S(2)}) async-start(bf16[128,4,128]{2,0,1:T(8,128)(2,1)} %copy_bitcast_fusion.2), calls=%async_computation | async-start | bytes 262144 | tf_op jit(solution)/shard_map/all_to_all | solution.py:69
  27.9 4.3 %copy-start.5 = (bf16[128,4,128]{2,0,1:T(8,128)(2,1)}, bf16[128,4,128]{2,0,1:T(8,128)(2,1)S(1)}, u32[]{:S(2)}) copy-start(bf16[128,4,128]{2,0,1:T(8,128)(2,1)S(1)} %all-to-all-done) | copy-start | bytes 393220
  27.9 7.9 %all-to-all-start.2 = ((bf16[128,4,128]{2,0,1:T(8,128)(2,1)}), bf16[128,4,128]{2,0,1:T(8,128)(2,1)S(1)}, u32[]{:S(2)}, u32[]{:S(2)}) async-start(bf16[128,4,128]{2,0,1:T(8,128)(2,1)} %bitcast.60), calls=%async_computation.2 | async-start | bytes 262144 | tf_op jit(solution)/shard_map/all_to_all | solution.py:70
  32.2 242.7 %all-gather.5.cloned.1.call-start = ((), (), s32[]{:S(2)}) async-start(), calls=%async_computation.6 | async-start | bytes 8519680 | tf_op jit(solution)/shard_map/all_gather | solution.py:85
  41.1 18.7 %copy-start.8 = (s32[1,1,12]{2,1,0:T(1,128)S(1)}, s32[1,1,12]{2,1,0:T(1,128)}, u32[]{:S(2)}) copy-start(s32[1,1,12]{2,1,0:T(1,128)} %param.14) | copy-start | bytes 148
  41.1 19.6 %copy-start.6 = (bf16[16,128,128]{2,1,0:T(8,128)(2,1)S(1)}, bf16[16,128,128]{2,1,0:T(8,128)(2,1)}, u32[]{:S(2)}) copy-start(bf16[16,128,128]{2,1,0:T(8,128)(2,1)} %param.15) | copy-start | bytes 1572868
  41.1 233.9 %all-to-all-start.3 = ((bf16[64,512,128]{2,1,0:T(8,128)(2,1)}), bf16[64,512,128]{2,1,0:T(8,128)(2,1)}, u32[]{:S(2)}, u32[]{:S(2)}) async-start(bf16[64,512,128]{2,1,0:T(8,128)(2,1)} %stack.23), calls=%async_computation.3 | async-start | bytes 16777216 | tf_op jit(solution)/shard_map/all_to_all | solution.py:87
  54.0 340.0 %all-gather.3.cloned.1.call-start = ((), (), s32[]{:S(2)}) async-start(), calls=%async_computation.5 | async-start | bytes 1966080 | tf_op jit(solution)/shard_map/all_gather | solution.py:54
  54.1 19.4 %collective-permute-start = (bf16[128,512]{1,0:T(8,128)(2,1)S(1)}, bf16[128,512]{1,0:T(8,128)(2,1)S(1)}, u32[]{:S(2)}, u32[]{:S(2)}) collective-permute-start(bf16[128,512]{1,0:T(8,128)(2,1)S(1)} %copy-done.1), channel_id=1, source_target_pairs={{0,4},{4,8},{8,12},{12,16},{16,20},{20,24},{24,28},{28,32},{32,36}... | collective-permute-start | bytes 393224 | tf_op jit(solution)/shard_map/ppermute | solution.py:19
  58.4 20.6 %collective-permute-start.1 = (bf16[128,512]{1,0:T(8,128)(2,1)S(1)}, bf16[128,512]{1,0:T(8,128)(2,1)S(1)}, u32[]{:S(2)}, u32[]{:S(2)}) collective-permute-start(bf16[128,512]{1,0:T(8,128)(2,1)S(1)} %copy-done.1), channel_id=1, source_target_pairs={{4,0},{8,4},{12,8},{16,12},{20,16},{24,20},{28,24},{32,28},{36,32}... | collective-permute-start | bytes 393224 | tf_op jit(solution)/shard_map/ppermute | solution.py:20
  389.0 8.8 %copy-start.4 = (bf16[512,512]{1,0:T(8,128)(2,1)S(1)}, bf16[512,512]{1,0:T(8,128)(2,1)}, u32[]{:S(2)}) copy-start(bf16[512,512]{1,0:T(8,128)(2,1)} %param.19) | copy-start | bytes 1572868
  389.0 9.1 %copy-start.2 = (bf16[1024,512]{1,0:T(8,128)(2,1)S(1)}, bf16[1024,512]{1,0:T(8,128)(2,1)}, u32[]{:S(2)}) copy-start(bf16[1024,512]{1,0:T(8,128)(2,1)} %param.21) | copy-start | bytes 3145732
  389.0 9.1 %copy-start.7 = (f32[512]{0:T(512)S(1)}, f32[512]{0:T(512)}, u32[]{:S(2)}) copy-start(f32[512]{0:T(512)} %param.23) | copy-start | bytes 6148
  389.8 7.8 %all-to-all-start.4 = ((bf16[4,128,128]{2,1,0:T(8,128)(2,1)}), bf16[4,128,128]{2,1,0:T(8,128)(2,1)S(1)}, u32[]{:S(2)}, u32[]{:S(2)}) async-start(bf16[4,128,128]{2,1,0:T(8,128)(2,1)} %bitcast.17), calls=%async_computation.4 | async-start | bytes 262144 | tf_op jit(solution)/shard_map/all_to_all | solution.py:124
Sparse Core Ops, SparseCore 0:
  36.7 238.2 all-gather.4
  276.8 28.0 all-gather.2
